TPU v7x, 512 devices: a whole 4x8x8 slice. The times are simulated.
512 devices in a mesh: src: 16 (over y, core), tgt: 32 (over x, z).
Axes of the slice: x: 4, y: 8, z: 8, core: 2. Of those that a mesh axis runs over, the one named last changes fastest.
Arguments:
- noise: float32 [16384, 384], P(('src', 'tgt')), may hold values from -16 to 16
- data: float32 [32768, 384], P('tgt', 'src'), may hold values from -6 to 6
Outputs:
- velocity: float32 [16384, 384], P(('src', 'tgt'))
- target_potential: float32 [32768], P('tgt')
All inputs are finite; a program needn't handle non-finite values.
Results may differ from a plain program's by a relative error of at most 0.0003.
Values sent between devices are 32-bit elements; how exact they have to be, the bound alone decides.
No kernel may reach another device: no remote copies, remote signals or barrier semaphores. Data moves between devices by JAX's collectives and lax.ppermute only.
A program may use at most 64 MiB of HBM per device.

v0:
```python
import math
import jax
import jax.numpy as jnp
from jax import lax
from jax.sharding import PartitionSpec as P

ITERS = 3
EPS = 0.05


def row_merge(z_tile):
    local_top = jnp.max(z_tile, axis=1)
    top = lax.pmax(local_top, "tgt")
    total = lax.psum(jnp.sum(jnp.exp(z_tile - top[:, None]), axis=1), "tgt")
    return top + jnp.log(total)


def col_merge(z_tile):
    local_top = jnp.max(z_tile, axis=0)
    top = lax.pmax(local_top, "src")
    total = lax.psum(jnp.sum(jnp.exp(z_tile - top[None, :]), axis=0), "src")
    return top + jnp.log(total)


def per_device(noise, data):
    source_rows = lax.all_gather(noise, "tgt", axis=0, tiled=True)
    target_rows = lax.all_gather(data, "src", axis=1, tiled=True)
    feat_width = source_rows.shape[1]
    src_total = source_rows.shape[0] * lax.axis_size("src")
    tgt_total = target_rows.shape[0] * lax.axis_size("tgt")
    source_sq = jnp.sum(source_rows * source_rows, axis=1)
    target_sq = jnp.sum(target_rows * target_rows, axis=1)
    cross = jnp.dot(
        source_rows,
        target_rows.T,
        precision=lax.Precision.HIGHEST,
        preferred_element_type=jnp.float32,
    )
    cost_tile = (source_sq[:, None] + target_sq[None, :] - 2.0 * cross) / feat_width
    g_pot = jnp.zeros((target_rows.shape[0],), jnp.float32)
    for step_index in range(ITERS):
        f_pot = -EPS * (math.log(src_total) + row_merge((g_pot[None, :] - cost_tile) / EPS))
        g_pot = -EPS * (math.log(tgt_total) + col_merge((f_pot[:, None] - cost_tile) / EPS))
    z_final = (g_pot[None, :] - cost_tile) / EPS
    lrow = row_merge(z_final)
    weight = jnp.exp(z_final - lrow[:, None])
    own_rows = noise.shape[0]
    whole = lax.psum(
        jnp.dot(
            weight, target_rows, precision=lax.Precision.HIGHEST, preferred_element_type=jnp.float32
        ),
        "tgt",
    )
    bary = lax.dynamic_slice_in_dim(whole, lax.axis_index("tgt") * own_rows, own_rows, 0)
    return (bary - noise, g_pot)


def solution(mesh):
    placed = (P(("src", "tgt"), None), P("tgt", "src"))
    return jax.shard_map(
        per_device,
        mesh=mesh,
        in_specs=placed,
        out_specs=(P(("src", "tgt"), None), P("tgt")),
        check_vma=False,
    )
```

profile of v0, /device:TPU:8, one launch (start us, length us, event | category | flops | bytes accessed | tf_op | source)
XLA Modules:
  0.0 1082.2 jit_solution(13867403295693776282)
XLA Ops:
  7.2 0.0 all-gather.5.cloned.1.call-start
  7.2 0.7 all-gather.5.cloned.1.call-update
  7.9 0.0 all-gather.3.cloned.1.call-start
  7.9 0.7 all-gather.3.cloned.1.call-update
  8.6 0.0 all-reduce.2.cloned.1.call-start
  8.7 47.0 %all-gather.5.cloned.1.call-done = f32[1024,384]{0,1:T(8,128)} async-done(((f32[1024,24]{0,1:T(8,128)}), f32[1024,384]{0,1:T(8,128)}) %all-gather.5.cloned.1.call-update) | async-done | bytes 1572880 | tf_op jit(solution)/shard_map/all_gather | solution.py:27
  55.7 1.5 multiply_reduce_fusion
  57.3 84.2 %all-gather.3.cloned.1.call-done = f32[1024,384]{1,0:T(8,128)} async-done(((f32[32,384]{1,0:T(8,128)}), f32[1024,384]{1,0:T(8,128)}) %all-gather.3.cloned.1.call-update) | async-done | bytes 1572880 | tf_op jit(solution)/shard_map/all_gather | solution.py:26
  141.5 1.6 multiply_reduce_fusion.1
  143.1 10.5 fusion.3
  153.6 72.1 %pmax.49 = f32[1024]{0:T(1024)S(1)} all-reduce(f32[1024]{0:T(1024)S(1)} %get-tuple-element.2), channel_id=1, replica_groups=mesh['src'=16,'tgt'=32] {'tgt'}, use_global_device_ids=true, to_apply=%region_3.0 | all-reduce | flops 1024 | bytes 8192 | tf_op jit(solution)/shard_map/pmax | solution.py:13
  225.7 3.0 exponential_reduce_fusion.6
  228.7 69.6 %psum.56 = f32[1024]{0:T(1024)S(1)} all-reduce(f32[1024]{0:T(1024)S(1)} %exponential_reduce_fusion.6), channel_id=1, replica_groups=mesh['src'=16,'tgt'=32] {'tgt'}, use_global_device_ids=true, to_apply=%region_5.0 | all-reduce | flops 1024 | bytes 8192 | tf_op jit(solution)/shard_map/psum | solution.py:14
  298.4 2.7 fusion.4
  301.1 20.6 %pmax.50 = f32[1024]{0:T(1024)S(1)} all-reduce(f32[1024]{0:T(1024)S(1)} %fusion.4), channel_id=1, replica_groups=mesh['src'=16,'tgt'=32] {'src'}, use_global_device_ids=true, to_apply=%region_7.0 | all-reduce | flops 1024 | bytes 8192 | tf_op jit(solution)/shard_map/pmax | solution.py:20
  321.7 3.2 exponential_reduce_fusion.5
  324.8 23.6 %psum.57 = f32[1024]{0:T(1024)S(1)} all-reduce(f32[1024]{0:T(1024)S(1)} %exponential_reduce_fusion.5), channel_id=1, replica_groups=mesh['src'=16,'tgt'=32] {'src'}, use_global_device_ids=true, to_apply=%region_9.0 | all-reduce | flops 1024 | bytes 8192 | tf_op jit(solution)/shard_map/psum | solution.py:21
  348.4 2.7 fusion.5
  351.1 71.6 %pmax.51 = f32[1024]{0:T(1024)S(1)} all-reduce(f32[1024]{0:T(1024)S(1)} %fusion.5), channel_id=1, replica_groups=mesh['src'=16,'tgt'=32] {'tgt'}, use_global_device_ids=true, to_apply=%region_11.0 | all-reduce | flops 1024 | bytes 8192 | tf_op jit(solution)/shard_map/pmax | solution.py:13
  422.7 3.1 exponential_reduce_fusion.4
  425.8 69.6 %psum.58 = f32[1024]{0:T(1024)S(1)} all-reduce(f32[1024]{0:T(1024)S(1)} %exponential_reduce_fusion.4), channel_id=1, replica_groups=mesh['src'=16,'tgt'=32] {'tgt'}, use_global_device_ids=true, to_apply=%region_13.0 | all-reduce | flops 1024 | bytes 8192 | tf_op jit(solution)/shard_map/psum | solution.py:14
  495.5 2.7 fusion.6
  498.1 23.6 %pmax.52 = f32[1024]{0:T(1024)S(1)} all-reduce(f32[1024]{0:T(1024)S(1)} %fusion.6), channel_id=1, replica_groups=mesh['src'=16,'tgt'=32] {'src'}, use_global_device_ids=true, to_apply=%region_15.0 | all-reduce | flops 1024 | bytes 8192 | tf_op jit(solution)/shard_map/pmax | solution.py:20
  521.7 3.2 exponential_reduce_fusion.3
  524.9 23.6 %psum.59 = f32[1024]{0:T(1024)S(1)} all-reduce(f32[1024]{0:T(1024)S(1)} %exponential_reduce_fusion.3), channel_id=1, replica_groups=mesh['src'=16,'tgt'=32] {'src'}, use_global_device_ids=true, to_apply=%region_17.0 | all-reduce | flops 1024 | bytes 8192 | tf_op jit(solution)/shard_map/psum | solution.py:21
  548.4 2.7 fusion.7
  551.1 71.8 %pmax.53 = f32[1024]{0:T(1024)S(1)} all-reduce(f32[1024]{0:T(1024)S(1)} %fusion.7), channel_id=1, replica_groups=mesh['src'=16,'tgt'=32] {'tgt'}, use_global_device_ids=true, to_apply=%region_19.0 | all-reduce | flops 1024 | bytes 8192 | tf_op jit(solution)/shard_map/pmax | solution.py:13
  622.9 3.1 exponential_reduce_fusion.2
  626.0 69.7 %psum.60 = f32[1024]{0:T(1024)S(1)} all-reduce(f32[1024]{0:T(1024)S(1)} %exponential_reduce_fusion.2), channel_id=1, replica_groups=mesh['src'=16,'tgt'=32] {'tgt'}, use_global_device_ids=true, to_apply=%region_21.0 | all-reduce | flops 1024 | bytes 8192 | tf_op jit(solution)/shard_map/psum | solution.py:14
  695.7 2.7 fusion.8
  698.3 23.6 %pmax.54 = f32[1024]{0:T(1024)S(1)} all-reduce(f32[1024]{0:T(1024)S(1)} %fusion.8), channel_id=1, replica_groups=mesh['src'=16,'tgt'=32] {'src'}, use_global_device_ids=true, to_apply=%region_23.0 | all-reduce | flops 1024 | bytes 8192 | tf_op jit(solution)/shard_map/pmax | solution.py:20
  721.9 3.2 exponential_reduce_fusion.1
  725.1 23.6 %psum.61 = f32[1024]{0:T(1024)S(1)} all-reduce(f32[1024]{0:T(1024)S(1)} %exponential_reduce_fusion.1), channel_id=1, replica_groups=mesh['src'=16,'tgt'=32] {'src'}, use_global_device_ids=true, to_apply=%region_25.0 | all-reduce | flops 1024 | bytes 8192 | tf_op jit(solution)/shard_map/psum | solution.py:21
  748.6 0.0 copy-start.2
  748.6 0.0 copy-start
  748.6 2.8 fusion.9
  751.4 71.6 %pmax.55 = f32[1024]{0:T(1024)S(1)} all-reduce(f32[1024]{0:T(1024)S(1)} %fusion.9), channel_id=1, replica_groups=mesh['src'=16,'tgt'=32] {'tgt'}, use_global_device_ids=true, to_apply=%region_27.0 | all-reduce | flops 1024 | bytes 8192 | tf_op jit(solution)/shard_map/pmax | solution.py:13
  823.0 3.1 exponential_reduce_fusion
  826.1 69.7 %psum.62 = f32[1024]{0:T(1024)S(1)} all-reduce(f32[1024]{0:T(1024)S(1)} %exponential_reduce_fusion), channel_id=1, replica_groups=mesh['src'=16,'tgt'=32] {'tgt'}, use_global_device_ids=true, to_apply=%region_29.0 | all-reduce | flops 1024 | bytes 8192 | tf_op jit(solution)/shard_map/psum | solution.py:14
  895.8 0.0 copy-done.2
  895.8 0.0 copy-done
  895.8 0.0 copy-start.1
  895.8 16.5 %fusion = f32[1024,384]{1,0:T(8,128)} fusion(f32[1024,384]{0,1:T(8,128)S(1)} %copy-done, f32[1024,1024]{0,1:T(8,128)} %get-tuple-element.3, f32[1024]{0:T(1024)S(1)} %log_add_fusion, f32[1024]{0:T(1024)S(1)} %add_multiply_fusion), kind=kOutput, calls=%fused_computation | convolution fusion | flops 4834983936 | bytes 7348224 | tf_op jit(solution)/shard_map/dot_general | solution.py:49
  912.3 0.0 all-reduce.2.cloned.1.call-update
  912.3 161.9 %all-reduce.2.cloned.1.call-done = f32[1024,384]{1,0:T(8,128)} async-done(((f32[1024,384]{1,0:T(8,128)}), f32[1024,384]{1,0:T(8,128)}) %all-reduce.2.cloned.1.call-update) | async-done | bytes 1572880 | tf_op jit(solution)/shard_map/psum | solution.py:48
  1074.2 0.0 copy-done.1
  1074.2 1.4 dynamic-slice_subtract_fusion
  (7 shorter events, 0.1 us)
Async XLA Ops:
  7.2 48.6 %all-gather.5.cloned.1.call-start = ((), (), s32[]{:S(2)}) async-start(), calls=%async_computation.1 | async-start | bytes 1671168 | tf_op jit(solution)/shard_map/all_gather | solution.py:27
  7.9 133.6 %all-gather.3.cloned.1.call-start = ((), (), s32[]{:S(2)}) async-start(), calls=%async_computation | async-start | bytes 1622016 | tf_op jit(solution)/shard_map/all_gather | solution.py:26
  8.6 1065.6 %all-reduce.2.cloned.1.call-start = ((), (), s32[]{:S(2)}) async-start(), calls=%async_computation.2 | async-start | bytes 3145728 | tf_op jit(solution)/shard_map/psum | solution.py:48
  748.6 147.2 %copy-start.2 = (f32[1024]{0:T(1024)}, f32[1024]{0:T(1024)S(1)}, u32[]{:S(2)}) copy-start(f32[1024]{0:T(1024)S(1)} %add_multiply_fusion) | copy-start | bytes 12292
  748.6 147.2 %copy-start = (f32[1024,384]{0,1:T(8,128)S(1)}, f32[1024,384]{0,1:T(8,128)}, u32[]{:S(2)}) copy-start(f32[1024,384]{0,1:T(8,128)} %all-gather.5.cloned.1.call-done) | copy-start | bytes 4718596
  895.8 178.4 %copy-start.1 = (f32[32,384]{1,0:T(8,128)S(1)}, f32[32,384]{1,0:T(8,128)}, u32[]{:S(2)}) copy-start(f32[32,384]{1,0:T(8,128)} %param.2) | copy-start | bytes 147460
Sparse Core Ops, SparseCore 0:
  10.1 45.5 all-gather.4
  58.9 82.5 all-gather.2
  912.5 161.7 all-reduce.1
where the time goes:
time: 1080 us
  blocking collectives  704 us (65%)
  waiting for transfers between devices  294 us (27%)
  other arithmetic  42.6 us (4%)
  matrix products  27 us (2%)
  between operations  13.9 us (1%)
    pmax x4, blocking collectives, row_merge(): top = lax.pmax(local_top, 'tgt')  287 us
    psum x4, blocking collectives, row_merge(): total = lax.psum(jnp.sum(jnp.exp(z_tile - top[:, None]), axis=1), 'tgt')  279 us
    psum x1, waiting for transfers between devices, per_device(): lax.psum(jnp.dot(weight, target_rows, precision=lax.Precision.HIGHEST, pr...  162 us
    all_gather x1, waiting for transfers between devices, per_device(): source_rows = lax.all_gather(noise, 'tgt', axis=0, tiled=True)  84.2 us
    psum x3, blocking collectives, col_merge(): total = lax.psum(jnp.sum(jnp.exp(z_tile - top[None, :]), axis=0), 'src')  70.7 us
    pmax x3, blocking collectives, col_merge(): top = lax.pmax(local_top, 'src')  67.7 us
    all_gather x1, waiting for transfers between devices, per_device(): target_rows = lax.all_gather(data, 'src', axis=1, tiled=True)  47 us
  transfers between devices with their start and end apart: 3, of which 3 were waited for; matrix products, arithmetic and copies ran while one was open for 0% of the time, Pallas kernels for 0%

commit v1 on v0

--- a/solution.py
+++ b/solution.py
@@ -1,3 +1,4 @@
+import functools
 import math
 import jax
 import jax.numpy as jnp
@@ -6,6 +7,16 @@
 
 ITERS = 3
 EPS = 0.05
+
+
+def return_all_routes_all_over_axis(view, where_dim):
+    reached = jnp.stack(lax.psum(1, "tgt") * [view], axis=0)
+    last = lax.all_to_all(reached, "tgt", 0, 0)
+    state_next = jnp.concatenate(last, axis=where_dim)
+    return state_next
+
+
+solve_domain = functools.partial(return_all_routes_all_over_axis, where_dim=0)
 
 
 def row_merge(z_tile):
@@ -23,7 +34,7 @@
 
 
 def per_device(noise, data):
-    source_rows = lax.all_gather(noise, "tgt", axis=0, tiled=True)
+    source_rows = solve_domain(noise)
     target_rows = lax.all_gather(data, "src", axis=1, tiled=True)
     feat_width = source_rows.shape[1]
     src_total = source_rows.shape[0] * lax.axis_size("src")

time: 1080 us -> 1000 us (0.926)
  waiting for transfers between devices: 294 us -> 200 us
  starting transfers between devices: 0.11 us -> 13.2 us
    all_gather x1 -> x0, waiting for transfers between devices: 84.2 us -> none  [per_device(): source_rows = lax.all_gather(noise, 'tgt', axis=0, tiled=True)]
    all_gather x1, waiting for transfers between devices: 47 us -> 32.3 us  [per_device(): target_rows = lax.all_gather(data, 'src', axis=1, tiled=True)]
    all_to_all x0 -> x1, starting transfers between devices: none -> 13.2 us  [return_all_routes_all_over_axis(): last = lax.all_to_all(reached, 'tgt', 0, 0)]
where the time goes in v1:
time: 1000 us
  blocking collectives  705 us (70%)
  waiting for transfers between devices  200 us (20%)
  other arithmetic  41.2 us (4%)
  matrix products  26.5 us (3%)
  between operations  14.2 us (1%)
  starting transfers between devices  13.2 us (1%)
    pmax x4, blocking collectives, row_merge(): top = lax.pmax(local_top, 'tgt')  287 us
    psum x4, blocking collectives, row_merge(): total = lax.psum(jnp.sum(jnp.exp(z_tile - top[:, None]), axis=1), 'tgt')  279 us
    psum x1, waiting for transfers between devices, per_device(): lax.psum(jnp.dot(weight, target_rows, precision=lax.Precision.HIGHEST, pr...  162 us
    psum x3, blocking collectives, col_merge(): total = lax.psum(jnp.sum(jnp.exp(z_tile - top[None, :]), axis=0), 'src')  71 us
    pmax x3, blocking collectives, col_merge(): top = lax.pmax(local_top, 'src')  67.8 us
    all_gather x1, waiting for transfers between devices, per_device(): target_rows = lax.all_gather(data, 'src', axis=1, tiled=True)  32.3 us
  transfers between devices with their start and end apart: 3, of which 3 were waited for; matrix products, arithmetic and copies ran while one was open for 0% of the time, Pallas kernels for 0%

profile of v1, /device:TPU:8, one launch (start us, length us, event | category | flops | bytes accessed | tf_op | source)
XLA Modules:
  0.0 1002.2 jit_solution(17835513098961187194)
XLA Ops:
  7.2 0.0 all-gather.2.cloned.1.call-start
  7.2 0.7 all-gather.2.cloned.1.call-update
  7.9 2.1 stack.2
  10.0 13.2 %all-to-all-start = ((f32[32,32,384]{2,1,0:T(8,128)}), f32[32,32,384]{2,1,0:T(8,128)S(1)}, u32[]{:S(2)}, u32[]{:S(2)}) async-start(f32[32,32,384]{2,1,0:T(8,128)} %stack.2), calls=%async_computation | async-start | bytes 3145728 | tf_op jit(solution)/shard_map/all_to_all | solution.py:14
  23.2 0.0 all-reduce.2.cloned.1.call-start
  23.3 32.3 %all-gather.2.cloned.1.call-done = f32[1024,384]{0,1:T(8,128)} async-done(((f32[1024,24]{0,1:T(8,128)}), f32[1024,384]{0,1:T(8,128)}) %all-gather.2.cloned.1.call-update) | async-done | bytes 1572880 | tf_op jit(solution)/shard_map/all_gather | solution.py:38
  55.6 1.5 multiply_reduce_fusion
  57.1 5.4 all-to-all-done
  62.5 0.2 multiply_reduce_fusion.1
  62.8 0.1 add.73
  62.8 10.0 fusion.3
  72.8 72.3 %pmax.49 = f32[1024]{0:T(1024)S(1)} all-reduce(f32[1024]{0:T(1024)S(1)} %get-tuple-element.2), channel_id=1, replica_groups=mesh['src'=16,'tgt'=32] {'tgt'}, use_global_device_ids=true, to_apply=%region_3.0 | all-reduce | flops 1024 | bytes 8192 | tf_op jit(solution)/shard_map/pmax | solution.py:24
  145.1 3.0 exponential_reduce_fusion.6
  148.2 69.6 %psum.56 = f32[1024]{0:T(1024)S(1)} all-reduce(f32[1024]{0:T(1024)S(1)} %exponential_reduce_fusion.6), channel_id=1, replica_groups=mesh['src'=16,'tgt'=32] {'tgt'}, use_global_device_ids=true, to_apply=%region_5.0 | all-reduce | flops 1024 | bytes 8192 | tf_op jit(solution)/shard_map/psum | solution.py:25
  217.8 2.7 fusion.4
  220.5 20.7 %pmax.50 = f32[1024]{0:T(1024)S(1)} all-reduce(f32[1024]{0:T(1024)S(1)} %fusion.4), channel_id=1, replica_groups=mesh['src'=16,'tgt'=32] {'src'}, use_global_device_ids=true, to_apply=%region_7.0 | all-reduce | flops 1024 | bytes 8192 | tf_op jit(solution)/shard_map/pmax | solution.py:31
  241.2 3.2 exponential_reduce_fusion.5
  244.3 23.9 %psum.57 = f32[1024]{0:T(1024)S(1)} all-reduce(f32[1024]{0:T(1024)S(1)} %exponential_reduce_fusion.5), channel_id=1, replica_groups=mesh['src'=16,'tgt'=32] {'src'}, use_global_device_ids=true, to_apply=%region_9.0 | all-reduce | flops 1024 | bytes 8192 | tf_op jit(solution)/shard_map/psum | solution.py:32
  268.2 2.7 fusion.5
  270.9 71.7 %pmax.51 = f32[1024]{0:T(1024)S(1)} all-reduce(f32[1024]{0:T(1024)S(1)} %fusion.5), channel_id=1, replica_groups=mesh['src'=16,'tgt'=32] {'tgt'}, use_global_device_ids=true, to_apply=%region_11.0 | all-reduce | flops 1024 | bytes 8192 | tf_op jit(solution)/shard_map/pmax | solution.py:24
  342.6 3.1 exponential_reduce_fusion.4
  345.7 69.6 %psum.58 = f32[1024]{0:T(1024)S(1)} all-reduce(f32[1024]{0:T(1024)S(1)} %exponential_reduce_fusion.4), channel_id=1, replica_groups=mesh['src'=16,'tgt'=32] {'tgt'}, use_global_device_ids=true, to_apply=%region_13.0 | all-reduce | flops 1024 | bytes 8192 | tf_op jit(solution)/shard_map/psum | solution.py:25
  415.3 2.7 fusion.6
  418.0 23.6 %pmax.52 = f32[1024]{0:T(1024)S(1)} all-reduce(f32[1024]{0:T(1024)S(1)} %fusion.6), channel_id=1, replica_groups=mesh['src'=16,'tgt'=32] {'src'}, use_global_device_ids=true, to_apply=%region_15.0 | all-reduce | flops 1024 | bytes 8192 | tf_op jit(solution)/shard_map/pmax | solution.py:31
  441.5 3.2 exponential_reduce_fusion.3
  444.7 23.6 %psum.59 = f32[1024]{0:T(1024)S(1)} all-reduce(f32[1024]{0:T(1024)S(1)} %exponential_reduce_fusion.3), channel_id=1, replica_groups=mesh['src'=16,'tgt'=32] {'src'}, use_global_device_ids=true, to_apply=%region_17.0 | all-reduce | flops 1024 | bytes 8192 | tf_op jit(solution)/shard_map/psum | solution.py:32
  468.3 2.7 fusion.7
  470.9 71.8 %pmax.53 = f32[1024]{0:T(1024)S(1)} all-reduce(f32[1024]{0:T(1024)S(1)} %fusion.7), channel_id=1, replica_groups=mesh['src'=16,'tgt'=32] {'tgt'}, use_global_device_ids=true, to_apply=%region_19.0 | all-reduce | flops 1024 | bytes 8192 | tf_op jit(solution)/shard_map/pmax | solution.py:24
  542.7 3.1 exponential_reduce_fusion.2
  545.8 69.7 %psum.60 = f32[1024]{0:T(1024)S(1)} all-reduce(f32[1024]{0:T(1024)S(1)} %exponential_reduce_fusion.2), channel_id=1, replica_groups=mesh['src'=16,'tgt'=32] {'tgt'}, use_global_device_ids=true, to_apply=%region_21.0 | all-reduce | flops 1024 | bytes 8192 | tf_op jit(solution)/shard_map/psum | solution.py:25
  615.5 2.7 fusion.8
  618.2 23.6 %pmax.54 = f32[1024]{0:T(1024)S(1)} all-reduce(f32[1024]{0:T(1024)S(1)} %fusion.8), channel_id=1, replica_groups=mesh['src'=16,'tgt'=32] {'src'}, use_global_device_ids=true, to_apply=%region_23.0 | all-reduce | flops 1024 | bytes 8192 | tf_op jit(solution)/shard_map/pmax | solution.py:31
  641.7 3.2 exponential_reduce_fusion.1
  644.9 23.6 %psum.61 = f32[1024]{0:T(1024)S(1)} all-reduce(f32[1024]{0:T(1024)S(1)} %exponential_reduce_fusion.1), channel_id=1, replica_groups=mesh['src'=16,'tgt'=32] {'src'}, use_global_device_ids=true, to_apply=%region_25.0 | all-reduce | flops 1024 | bytes 8192 | tf_op jit(solution)/shard_map/psum | solution.py:32
  668.5 0.0 copy-start.2
  668.5 0.0 copy-start
  668.5 2.8 fusion.9
  671.3 71.6 %pmax.55 = f32[1024]{0:T(1024)S(1)} all-reduce(f32[1024]{0:T(1024)S(1)} %fusion.9), channel_id=1, replica_groups=mesh['src'=16,'tgt'=32] {'tgt'}, use_global_device_ids=true, to_apply=%region_27.0 | all-reduce | flops 1024 | bytes 8192 | tf_op jit(solution)/shard_map/pmax | solution.py:24
  742.9 3.1 exponential_reduce_fusion
  746.0 69.7 %psum.62 = f32[1024]{0:T(1024)S(1)} all-reduce(f32[1024]{0:T(1024)S(1)} %exponential_reduce_fusion), channel_id=1, replica_groups=mesh['src'=16,'tgt'=32] {'tgt'}, use_global_device_ids=true, to_apply=%region_29.0 | all-reduce | flops 1024 | bytes 8192 | tf_op jit(solution)/shard_map/psum | solution.py:25
  815.6 0.0 copy-done.2
  815.6 0.0 copy-done
  815.6 0.0 copy-start.1
  815.7 16.5 %fusion = f32[1024,384]{1,0:T(8,128)} fusion(f32[1024,384]{0,1:T(8,128)S(1)} %copy-done, f32[1024,1024]{0,1:T(8,128)} %get-tuple-element.3, f32[1024]{0:T(1024)S(1)} %log_add_fusion, f32[1024]{0:T(1024)S(1)} %add_multiply_fusion), kind=kOutput, calls=%fused_computation | convolution fusion | flops 4834983936 | bytes 7348224 | tf_op jit(solution)/shard_map/dot_general | solution.py:60
  832.1 0.0 all-reduce.2.cloned.1.call-update
  832.2 161.7 %all-reduce.2.cloned.1.call-done = f32[1024,384]{1,0:T(8,128)} async-done(((f32[1024,384]{1,0:T(8,128)}), f32[1024,384]{1,0:T(8,128)}) %all-reduce.2.cloned.1.call-update) | async-done | bytes 1572880 | tf_op jit(solution)/shard_map/psum | solution.py:59
  993.9 0.0 copy-done.1
  993.9 1.4 dynamic-slice_subtract_fusion
  (7 shorter events, 0.1 us)
Async XLA Ops:
  7.2 48.4 %all-gather.2.cloned.1.call-start = ((), (), s32[]{:S(2)}) async-start(), calls=%async_computation.1 | async-start | bytes 1671168 | tf_op jit(solution)/shard_map/all_gather | solution.py:38
  10.0 52.5 %all-to-all-start = ((f32[32,32,384]{2,1,0:T(8,128)}), f32[32,32,384]{2,1,0:T(8,128)S(1)}, u32[]{:S(2)}, u32[]{:S(2)}) async-start(f32[32,32,384]{2,1,0:T(8,128)} %stack.2), calls=%async_computation | async-start | bytes 3145728 | tf_op jit(solution)/shard_map/all_to_all | solution.py:14
  23.2 970.7 %all-reduce.2.cloned.1.call-start = ((), (), s32[]{:S(2)}) async-start(), calls=%async_computation.2 | async-start | bytes 3145728 | tf_op jit(solution)/shard_map/psum | solution.py:59
  668.5 147.2 %copy-start.2 = (f32[1024]{0:T(1024)}, f32[1024]{0:T(1024)S(1)}, u32[]{:S(2)}) copy-start(f32[1024]{0:T(1024)S(1)} %add_multiply_fusion) | copy-start | bytes 12292
  668.5 147.2 %copy-start = (f32[1024,384]{0,1:T(8,128)S(1)}, f32[1024,384]{0,1:T(8,128)}, u32[]{:S(2)}) copy-start(f32[1024,384]{0,1:T(8,128)} %all-gather.2.cloned.1.call-done) | copy-start | bytes 4718596
  815.6 178.2 %copy-start.1 = (f32[32,384]{1,0:T(8,128)S(1)}, f32[32,384]{1,0:T(8,128)}, u32[]{:S(2)}) copy-start(f32[32,384]{1,0:T(8,128)} %param.2) | copy-start | bytes 147460
Sparse Core Ops, SparseCore 0:
  10.1 45.4 all-gather.1
  832.3 161.5 all-reduce.1
